TPU v7x, 32 devices: a whole 2x2x4 slice. The times are simulated.
32 devices in a mesh: dp: 16 (over z, x, core), tensor: 2 (over y).
Axes of the slice: x: 2, y: 2, z: 4, core: 2. Of those that a mesh axis runs over, the one named last changes fastest.
Arguments:
- inputs: bfloat16 [6272, 512], P('dp'), may hold values from -6 to 6
- ln1_gain: float32 [512], replicated, may hold values from 0.5 to 1.5
- ln1_shift: float32 [512], replicated, may hold values from -3 to 3
- w_qkv: bfloat16 [512, 3, 512], P(None, None, 'tensor'), may hold values from -0.25 to 0.25
- qv_bias: float32 [2, 512], P(None, 'tensor'), may hold values from -3 to 3
- bias_table: float32 [169, 16], P(None, 'tensor'), may hold values from -6 to 320
- rel_index: int32 [49, 49], replicated, may hold values from 0 to 168
- regions: int32 [196], replicated, may hold values from 0 to 8
- w_proj: bfloat16 [512, 512], P('tensor'), may hold values from -0.5 to 0.5
- proj_bias: float32 [512], replicated, may hold values from -3 to 3
- ln2_gain: float32 [512], replicated, may hold values from 0.5 to 1.5
- ln2_shift: float32 [512], replicated, may hold values from -3 to 3
- w_fc1: bfloat16 [512, 2048], P(None, 'tensor'), may hold values from -0.25 to 0.25
- fc1_bias: float32 [2048], P('tensor'), may hold values from -3 to 3
- w_fc2: bfloat16 [2048, 512], P('tensor'), may hold values from -0.1875 to 0.1875
- fc2_bias: float32 [512], replicated, may hold values from -3 to 3
- grad_output: bfloat16 [6272, 512], P('dp'), may hold values from -12 to 12
Outputs:
- output: bfloat16 [6272, 512], P('dp')
- grad_input: float32 [6272, 512], P('dp')
- grad_ln1_gain: float32 [512], replicated
- grad_ln1_shift: float32 [512], replicated
- grad_qkv: float32 [512, 3, 512], P(None, None, 'tensor')
- grad_qv_bias: float32 [2, 512], P(None, 'tensor')
- grad_table: float32 [169, 16], P(None, 'tensor')
- grad_proj: float32 [512, 512], P('tensor')
- grad_proj_bias: float32 [512], replicated
- grad_ln2_gain: float32 [512], replicated
- grad_ln2_shift: float32 [512], replicated
- grad_fc1: float32 [512, 2048], P(None, 'tensor')
- grad_fc1_bias: float32 [2048], P('tensor')
- grad_fc2: float32 [2048, 512], P('tensor')
- grad_fc2_bias: float32 [512], replicated
All inputs are finite; a program needn't handle non-finite values.
Results may differ from a plain program's by a relative error of at most 0.017.
Values may be sent and summed in bfloat16 or wider, within the bound.
No kernel may reach another device: no remote copies, remote signals or barrier semaphores. Data moves between devices by JAX's collectives and lax.ppermute only.
A program may use at most 64 MiB of HBM per device.

v0:
```python
import jax
import jax.numpy as jnp
from jax import lax
from jax.sharding import PartitionSpec as P

HEAD_DIM = 32
SIDE = 14
WIN = 7
SHIFT = 3
NORM_EPS = 1e-05
MASKED = -1e30


def layer_norm(values, norm_gain, norm_shift):
    centered = values - jnp.mean(values, axis=-1, keepdims=True)
    inverse = lax.rsqrt(jnp.mean(centered * centered, axis=-1, keepdims=True) + NORM_EPS)
    normed = centered * inverse
    return (normed * norm_gain + norm_shift, normed, inverse)


def norm_backward(upstream, normed, inverse, norm_gain):
    weighted = upstream * norm_gain
    return inverse * (
        weighted
        - jnp.mean(weighted, axis=-1, keepdims=True)
        - normed * jnp.mean(weighted * normed, axis=-1, keepdims=True)
    )


def gelu_exact(hidden):
    return 0.5 * hidden * (1.0 + jax.scipy.special.erf(hidden * 0.7071067811865476))


def gelu_slope(hidden):
    return (
        0.5 * (1.0 + jax.scipy.special.erf(hidden * 0.7071067811865476))
        + hidden * jnp.exp(-0.5 * hidden * hidden) * 0.3989422804014327
    )


def to_windows(tensor, images):
    heads_here = tensor.shape[1]
    head_depth = tensor.shape[2]
    across = SIDE // WIN
    layout = tensor.reshape(images, SIDE, SIDE, heads_here, head_depth)
    layout = jnp.roll(layout, (-SHIFT, -SHIFT), axis=(1, 2))
    layout = layout.reshape(images, across, WIN, across, WIN, heads_here, head_depth).transpose(
        0, 1, 3, 5, 2, 4, 6
    )
    return layout.reshape(images * across * across, heads_here, WIN * WIN, head_depth)


def from_windows(tensor, images):
    heads_here = tensor.shape[1]
    head_depth = tensor.shape[3]
    across = SIDE // WIN
    layout = tensor.reshape(images, across, across, heads_here, WIN, WIN, head_depth).transpose(
        0, 1, 4, 2, 5, 3, 6
    )
    layout = jnp.roll(
        layout.reshape(images, SIDE, SIDE, heads_here, head_depth), (SHIFT, SHIFT), axis=(1, 2)
    )
    return layout.reshape(images * SIDE * SIDE, heads_here * head_depth)


def window_scores(queries, keys_win, rel_bias, allowed, images):
    raw_scores = jnp.einsum(
        "whie,whje->whij", queries, keys_win, preferred_element_type=jnp.float32
    )
    layout = (
        raw_scores.reshape((images, allowed.shape[0]) + raw_scores.shape[1:]) + rel_bias[None, None]
    )
    return jnp.where(allowed[None, :, None], layout, MASKED)


def local(
    inputs,
    ln1_gain,
    ln1_shift,
    w_qkv,
    qv_bias,
    bias_table,
    rel_index,
    regions,
    w_proj,
    proj_bias,
    ln2_gain,
    ln2_shift,
    w_fc1,
    fc1_bias,
    w_fc2,
    fc2_bias,
    grad_output,
):
    tokens_here = inputs.shape[0]
    width = inputs.shape[1]
    images = tokens_here // (SIDE * SIDE)
    inner = w_qkv.shape[2]
    heads_here = inner // HEAD_DIM
    q_factor = HEAD_DIM ** (-0.5)
    across = SIDE // WIN
    positions = WIN * WIN
    residual_in = inputs.astype(jnp.float32)
    normed_one, unit_one, inverse_one = layer_norm(residual_in, ln1_gain, ln1_shift)
    normed_one_b = normed_one.astype(jnp.bfloat16)
    qkv_weight = w_qkv.reshape(width, 3 * inner)
    projected = jnp.dot(normed_one_b, qkv_weight, preferred_element_type=jnp.float32).reshape(
        tokens_here, 3, inner
    )
    queries = ((projected[:, 0] + qv_bias[0]) * q_factor).astype(jnp.bfloat16)
    keys_tok = projected[:, 1].astype(jnp.bfloat16)
    values_tok = (projected[:, 2] + qv_bias[1]).astype(jnp.bfloat16)
    query_win = to_windows(queries.reshape(tokens_here, heads_here, HEAD_DIM), images)
    key_win = to_windows(keys_tok.reshape(tokens_here, heads_here, HEAD_DIM), images)
    value_win = to_windows(values_tok.reshape(tokens_here, heads_here, HEAD_DIM), images)
    region_win = (
        regions.reshape(across, WIN, across, WIN)
        .transpose(0, 2, 1, 3)
        .reshape(across * across, positions)
    )
    allowed = region_win[:, :, None] == region_win[:, None, :]
    one_hot = (
        rel_index.reshape(-1)[:, None] == jnp.arange(bias_table.shape[0], dtype=jnp.int32)[None, :]
    ).astype(jnp.float32)
    rel_bias = jnp.dot(one_hot, bias_table, precision=lax.Precision.HIGHEST).T.reshape(
        heads_here, positions, positions
    )
    scores = window_scores(query_win, key_win, rel_bias, allowed, images)
    top_score = jnp.max(scores, axis=-1, keepdims=True)
    log_total = top_score + jnp.log(jnp.sum(jnp.exp(scores - top_score), axis=-1, keepdims=True))
    prob_b = (
        jnp.exp(scores - log_total)
        .astype(jnp.bfloat16)
        .reshape(-1, heads_here, positions, positions)
    )
    mixed = jnp.einsum("whij,whje->whie", prob_b, value_win, preferred_element_type=jnp.float32)
    mixed_tok = from_windows(mixed.astype(jnp.bfloat16), images)
    attn_part = jnp.dot(mixed_tok, w_proj, preferred_element_type=jnp.float32)
    attn_total = lax.psum(attn_part.astype(jnp.bfloat16), "tensor").astype(jnp.float32)
    hidden_res = residual_in + attn_total + proj_bias
    normed_two, unit_two, inverse_two = layer_norm(hidden_res, ln2_gain, ln2_shift)
    normed_two_b = normed_two.astype(jnp.bfloat16)
    pre_act = jnp.dot(normed_two_b, w_fc1, preferred_element_type=jnp.float32) + fc1_bias
    activ_b = gelu_exact(pre_act).astype(jnp.bfloat16)
    mlp_part = jnp.dot(activ_b, w_fc2, preferred_element_type=jnp.float32)
    mlp_total = lax.psum(mlp_part.astype(jnp.bfloat16), "tensor").astype(jnp.float32)
    output = (hidden_res + mlp_total + fc2_bias).astype(jnp.bfloat16)
    upstream = grad_output.astype(jnp.float32)
    grad_fc2_bias = jnp.sum(upstream, axis=0)
    grad_fc2 = jnp.dot(activ_b.T, grad_output, preferred_element_type=jnp.float32)
    grad_act = jnp.dot(grad_output, w_fc2.T, preferred_element_type=jnp.float32)
    grad_pre = grad_act * gelu_slope(pre_act)
    grad_pre_b = grad_pre.astype(jnp.bfloat16)
    grad_fc1_bias = jnp.sum(grad_pre, axis=0)
    grad_fc1 = jnp.dot(normed_two_b.T, grad_pre_b, preferred_element_type=jnp.float32)
    back_two_part = jnp.dot(grad_pre_b, w_fc1.T, preferred_element_type=jnp.float32)
    back_two = lax.psum(back_two_part.astype(jnp.bfloat16), "tensor").astype(jnp.float32)
    grad_ln2_gain = jnp.sum(back_two * unit_two, axis=0)
    grad_ln2_shift = jnp.sum(back_two, axis=0)
    mlp_sums = (grad_ln2_gain, grad_ln2_shift, grad_fc1, grad_fc1_bias, grad_fc2, grad_fc2_bias)
    grad_hidden = upstream + norm_backward(back_two, unit_two, inverse_two, ln2_gain)
    grad_hidden_b = grad_hidden.astype(jnp.bfloat16)
    grad_proj_bias = jnp.sum(grad_hidden, axis=0)
    grad_proj = jnp.dot(mixed_tok.T, grad_hidden_b, preferred_element_type=jnp.float32)
    grad_mixed = jnp.dot(grad_hidden_b, w_proj.T, preferred_element_type=jnp.float32).astype(
        jnp.bfloat16
    )
    grad_mixed_win = to_windows(grad_mixed.reshape(tokens_here, heads_here, HEAD_DIM), images)
    scores_again = window_scores(query_win, key_win, rel_bias, allowed, images)
    prob_again = jnp.exp(scores_again - log_total)
    prob_again_b = prob_again.astype(jnp.bfloat16).reshape(-1, heads_here, positions, positions)
    grad_prob = jnp.einsum(
        "whie,whje->whij", grad_mixed_win, value_win, preferred_element_type=jnp.float32
    ).reshape(prob_again.shape)
    row_dot = jnp.sum(prob_again * grad_prob, axis=-1, keepdims=True)
    grad_score = prob_again * (grad_prob - row_dot)
    summed_scores = jnp.sum(grad_score, axis=(0, 1)).reshape(heads_here, positions * positions)
    grad_table = jnp.dot(one_hot.T, summed_scores.T, precision=lax.Precision.HIGHEST)
    grad_score_b = grad_score.astype(jnp.bfloat16).reshape(-1, heads_here, positions, positions)
    grad_query_win = (
        jnp.einsum("whij,whje->whie", grad_score_b, key_win, preferred_element_type=jnp.float32)
        * q_factor
    )
    grad_key_win = jnp.einsum(
        "whij,whie->whje", grad_score_b, query_win, preferred_element_type=jnp.float32
    )
    grad_value_win = jnp.einsum(
        "whij,whie->whje", prob_again_b, grad_mixed_win, preferred_element_type=jnp.float32
    )
    grad_query = from_windows(grad_query_win, images)
    grad_key = from_windows(grad_key_win, images)
    grad_value = from_windows(grad_value_win, images)
    grad_qv_bias = jnp.stack([jnp.sum(grad_query, axis=0), jnp.sum(grad_value, axis=0)])
    grad_three = (
        jnp.stack([grad_query, grad_key, grad_value], axis=1)
        .astype(jnp.bfloat16)
        .reshape(tokens_here, 3 * inner)
    )
    grad_qkv = jnp.dot(normed_one_b.T, grad_three, preferred_element_type=jnp.float32).reshape(
        width, 3, inner
    )
    back_one_part = jnp.dot(grad_three, qkv_weight.T, preferred_element_type=jnp.float32)
    back_one = lax.psum(back_one_part.astype(jnp.bfloat16), "tensor").astype(jnp.float32)
    grad_ln1_gain = jnp.sum(back_one * unit_one, axis=0)
    grad_ln1_shift = jnp.sum(back_one, axis=0)
    grad_input = grad_hidden + norm_backward(back_one, unit_one, inverse_one, ln1_gain)
    total_grads = tuple(
        lax.psum(
            (
                grad_ln1_gain,
                grad_ln1_shift,
                grad_qkv,
                grad_qv_bias,
                grad_table,
                grad_proj,
                grad_proj_bias,
                mlp_sums[0],
                mlp_sums[1],
                mlp_sums[2],
                mlp_sums[3],
                mlp_sums[4],
                mlp_sums[5],
            ),
            "dp",
        )
    )
    return (output, grad_input) + total_grads


def solution(mesh):
    return jax.shard_map(
        local,
        mesh=mesh,
        in_specs=(
            P("dp", None),
            P(),
            P(),
            P(None, None, "tensor"),
            P(None, "tensor"),
            P(None, "tensor"),
            P(),
            P(),
            P("tensor", None),
            P(),
            P(),
            P(),
            P(None, "tensor"),
            P("tensor"),
            P("tensor", None),
            P(),
            P("dp", None),
        ),
        out_specs=(
            P("dp", None),
            P("dp", None),
            P(),
            P(),
            P(None, None, "tensor"),
            P(None, "tensor"),
            P(None, "tensor"),
            P("tensor", None),
            P(),
            P(),
            P(),
            P(None, "tensor"),
            P("tensor"),
            P("tensor", None),
            P(),
        ),
        check_vma=False,
    )
```

profile of v0, /device:TPU:0, one launch (start us, length us, event | category | flops | bytes accessed | tf_op | source)
XLA Modules:
  0.0 338.9 jit_solution(2142861799854349741)
XLA Ops:
  7.3 1.2 convert_reduce_fusion.2
  8.5 1.2 fusion.26
  9.8 1.4 copy.96
  13.7 0.9 slice.167
  14.7 1.4 squeeze.7
  16.9 0.9 slice.162
  18.4 0.9 slice.172
  19.8 1.2 convolution_bitcast_fusion
  21.2 0.8 copy.101
  22.4 1.3 copy.100
  24.2 1.4 copy.99
  25.6 2.0 fusion.72
  28.9 0.9 copy.102
  29.9 2.4 copy.104
  32.3 2.2 convolution_convert_fusion
  34.5 2.4 copy.105
  37.0 1.2 copy.106
  38.2 1.1 fusion.35
  39.3 1.7 reshape.250
  41.1 2.0 convolution_convert_fusion.3
  43.4 28.6 %all-reduce.8.cloned.1.call-done = bf16[392,512]{1,0:T(8,128)(2,1)} async-done(((bf16[392,512]{1,0:T(8,128)(2,1)}), bf16[392,512]{1,0:T(8,128)(2,1)}) %all-reduce.8.cloned.1.call-update) | async-done | bytes 401424 | tf_op jit(solution)/shard_map/psum | solution.py:139
  72.0 1.3 fusion.55
  73.3 1.3 multiply_reduce_fusion.1
  74.7 1.8 multiply_convert_fusion
  76.5 1.6 fusion.73
  78.1 0.9 copy-done.58
  78.9 1.4 convolution_convert_fusion.1
  80.4 2.9 convolution_convert_fusion.2
  83.3 2.2 fusion.52
  85.6 21.0 %all-reduce.10.cloned.1.call-done = bf16[392,512]{1,0:T(8,128)(2,1)} async-done(((bf16[392,512]{1,0:T(8,128)(2,1)}), bf16[392,512]{1,0:T(8,128)(2,1)}) %all-reduce.10.cloned.1.call-update) | async-done | bytes 401424 | tf_op jit(solution)/shard_map/psum | solution.py:157
  106.6 2.2 fusion.32
  108.8 2.3 fusion.65
  111.4 1.2 reshape_reshape.2
  112.6 0.9 slice.179
  113.6 1.1 slice.178
  115.0 0.9 copy.107
  116.0 2.4 copy.108
  118.4 2.6 fusion.56
  121.0 3.0 copy.120
  124.1 1.5 copy.121
  126.4 1.1 slice.187
  128.3 1.3 fusion.66
  130.6 1.4 convolution_multiply_fusion
  132.7 0.9 slice.185
  133.5 1.9 copy.112
  135.7 1.2 copy-done.3
  136.9 0.8 fusion.68
  139.0 1.2 stack_reshape.10
  140.2 1.1 pad_maximum_fusion.2
  142.6 2.5 fusion.8
  145.5 2.1 fusion.74
  147.6 1.1 fusion.59
  148.7 1.9 fusion.45
  150.7 0.8 copy-done.25
  152.0 0.9 fusion
  152.9 27.3 %all-reduce.14.cloned.1.call-done = (bf16[392,512]{1,0:T(8,128)(2,1)}, bf16[392,512]{1,0:T(8,128)(2,1)}) async-done(((bf16[392,512]{1,0:T(8,128)(2,1)}, bf16[392,512]{1,0:T(8,128)(2,1)}), (bf16[392,512]{1,0:T(8,128)(2,1)}, bf16[392,512]{1,0:T(8,128)(2,1)})) %all-reduce.14.cloned.1.call-update) | async-done | bytes 802832 | tf_op jit(solution)/shard_map/psum | solution.py:146
  180.2 1.5 fusion.33
  181.8 63.3 %all-reduce = (f32[512]{0:T(512)}, f32[512]{0:T(512)}, f32[2,256]{1,0:T(2,128)}, f32[169,8]{0,1:T(8,128)}, f32[512]{0:T(512)}, /*index=5*/f32[512]{0:T(512)}, f32[512]{0:T(512)}, f32[1024]{0:T(1024)}, f32[512]{0:T(512)}) all-reduce(f32[512]{0:T(512)S(1)} %get-tuple-element.17, ...), channel_id=1, replica_groups=mesh['dp'=16,'tensor'=2] {'dp'}, use_global_device_ids=true, to_apply=%region_16.17 | all-reduce | flops 5960 | bytes 47680 | tf_op jit(solution)/shard_map/psum | solution.py:208
  245.1 2.6 fusion.25
  247.7 77.4 %all-reduce.12.cloned.1.call-done = (f32[512,3,256]{2,0,1:T(8,128)}, f32[256,512]{1,0:T(8,128)}, f32[512,1024]{1,0:T(8,128)}, f32[1024,512]{1,0:T(8,128)}) async-done(((f32[512,3,256]{2,0,1:T(8,128)}, f32[256,512]{1,0:T(8,128)}, f32[512,1024]{1,0:T(8,128)}, f32[1024,512]{1,0:T(8,128)}), (f32[512,3,256]{2,0,1:T(8,128)}, f32[256,512]{1,0:T(8,128)}, f32[512,1024]{1,0:T(8,128)}, ...) | async-done | bytes 6291472 | tf_op jit(solution)/shard_map/psum | solution.py:208
  325.1 2.8 copy.146
  328.7 1.3 copy.148
  330.0 1.0 copy-done.16
  331.0 1.3 copy.149
  (189 shorter events, 15.5 us)
Async XLA Ops:
  7.2 67.4 %copy-start = (bf16[512,1024]{1,0:T(8,128)(2,1)S(1)}, bf16[512,1024]{1,0:T(8,128)(2,1)}, u32[]{:S(2)}) copy-start(bf16[512,1024]{1,0:T(8,128)(2,1)} %param.29) | copy-start | bytes 3145732
  7.2 4.0 %copy-start.2 = (bf16[392,512]{1,0:T(8,128)(2,1)S(1)}, bf16[392,512]{1,0:T(8,128)(2,1)}, u32[]{:S(2)}) copy-start(bf16[392,512]{1,0:T(8,128)(2,1)} %param.17) | copy-start | bytes 1204228
  7.2 4.0 %copy-start.42 = (f32[512]{0:T(512)S(1)}, f32[512]{0:T(512)}, u32[]{:S(2)}) copy-start(f32[512]{0:T(512)} %param.18) | copy-start | bytes 6148
  7.2 4.0 %copy-start.56 = (f32[512]{0:T(512)S(1)}, f32[512]{0:T(512)}, u32[]{:S(2)}) copy-start(f32[512]{0:T(512)} %param.19) | copy-start | bytes 6148
  7.2 64.8 %all-reduce.8.cloned.1.call-start = ((), (), s32[]{:S(2)}) async-start(), calls=%async_computation | async-start | bytes 802816 | tf_op jit(solution)/shard_map/psum | solution.py:139
  9.8 2.0 copy-start.35
  12.7 1.9 copy-start.50
  18.2 1.1 copy-start.34
  18.2 1.2 copy-start.51
  18.3 1.5 copy-start.53
  18.4 3.6 %copy-start.8 = (bf16[2,11,14,8,32]{4,3,2,1,0:T(8,128)(2,1)S(1)}, bf16[2,11,14,8,32]{4,3,2,1,0:T(8,128)(2,1)}, u32[]{:S(2)}) copy-start(bf16[2,11,14,8,32]{4,3,2,1,0:T(8,128)(2,1)} %slice.167) | copy-start | bytes 473092
  18.4 3.6 %copy-start.22 = (bf16[2,3,14,8,32]{4,3,2,1,0:T(8,128)(2,1)S(1)}, bf16[2,3,14,8,32]{4,3,2,1,0:T(8,128)(2,1)}, u32[]{:S(2)}) copy-start(bf16[2,3,14,8,32]{4,3,2,1,0:T(8,128)(2,1)} %slice.168) | copy-start | bytes 129028
  19.4 2.9 copy-start.38
  22.3 1.4 copy-start.9
  22.4 1.4 copy-start.23
  27.5 1.1 copy-start.7
  28.6 3.7 %copy-start.26 = (f32[8,8,49]{2,1,0:T(8,128)}, f32[8,8,49]{2,1,0:T(8,128)S(1)}, u32[]{:S(2)}) copy-start(f32[8,8,49]{2,1,0:T(8,128)S(1)} %log_add_fusion) | copy-start | bytes 37636
  38.2 33.8 %copy-start.32 = (f32[512]{0:T(512)S(1)}, f32[512]{0:T(512)}, u32[]{:S(2)}) copy-start(f32[512]{0:T(512)} %param.26) | copy-start | bytes 6148
  41.0 35.4 %copy-start.18 = (bf16[392,256]{1,0:T(8,128)(2,1)}, bf16[392,256]{1,0:T(8,128)(2,1)S(1)}, u32[]{:S(2)}) copy-start(bf16[392,256]{1,0:T(8,128)(2,1)S(1)} %reshape.250) | copy-start | bytes 602116
  41.1 33.6 %copy-start.40 = (f32[512]{0:T(512)S(1)}, f32[512]{0:T(512)}, u32[]{:S(2)}) copy-start(f32[512]{0:T(512)} %param.27) | copy-start | bytes 6148
  41.1 33.6 %copy-start.54 = (f32[1024]{0:T(1024)S(1)}, f32[1024]{0:T(1024)}, u32[]{:S(2)}) copy-start(f32[1024]{0:T(1024)} %param.30) | copy-start | bytes 12292
  41.1 33.6 %copy-start.55 = (f32[512]{0:T(512)S(1)}, f32[512]{0:T(512)}, u32[]{:S(2)}) copy-start(f32[512]{0:T(512)} %param.28) | copy-start | bytes 6148
  43.2 63.4 %all-reduce.10.cloned.1.call-start = ((), (), s32[]{:S(2)}) async-start(), calls=%async_computation.1 | async-start | bytes 802816 | tf_op jit(solution)/shard_map/psum | solution.py:157
  72.0 2.6 copy-start.4
  73.3 10.0 %copy-start.33 = (f32[392]{0:T(512)}, f32[392]{0:T(512)S(1)}, u32[]{:S(2)}) copy-start(f32[392]{0:T(512)S(1)} %broadcast_multiply_fusion.4) | copy-start | bytes 4708
  74.7 8.6 %copy-start.37 = (f32[392]{0:T(512)}, f32[392]{0:T(512)S(1)}, u32[]{:S(2)}) copy-start(f32[392]{0:T(512)S(1)} %add_rsqrt_fusion) | copy-start | bytes 4708
  74.7 1.8 copy-start.20
  74.7 1.8 copy-start.52
  78.1 0.9 copy-start.58
  80.3 3.0 copy-start.5
  80.3 99.9 %all-reduce.14.cloned.1.call-start = ((), (), s32[]{:S(2)}) async-start(), calls=%async_computation.3 | async-start | bytes 1605632 | tf_op jit(solution)/shard_map/psum | solution.py:146
  80.4 2.9 copy-start.59
  83.3 23.3 %copy-start.41 = (f32[512]{0:T(512)S(1)}, f32[512]{0:T(512)}, u32[]{:S(2)}) copy-start(f32[512]{0:T(512)} %param.27) | copy-start | bytes 6148
  85.6 25.5 %copy-start.24 = (bf16[256,512]{1,0:T(8,128)(2,1)S(1)}, bf16[256,512]{1,0:T(8,128)(2,1)}, u32[]{:S(2)}) copy-start(bf16[256,512]{1,0:T(8,128)(2,1)} %param.25) | copy-start | bytes 786436
  115.0 3.4 %copy-start.27 = (f32[8,8,49]{2,1,0:T(8,128)S(1)}, f32[8,8,49]{2,1,0:T(8,128)}, u32[]{:S(2)}) copy-start(f32[8,8,49]{2,1,0:T(8,128)} %copy-done.26) | copy-start | bytes 37636
  125.6 1.9 copy-start.12
  125.6 1.9 copy-start.13
  128.3 1.3 copy-start.11
  129.6 1.0 copy-start.10
  135.6 1.3 copy-start.3
  135.6 1.3 copy-start.14
  137.7 1.1 copy-start.15
  139.0 2.9 copy-start.29
  141.3 1.3 copy-start.31
  142.6 2.9 copy-start.21
  142.6 2.9 copy-start.28
  145.2 2.4 copy-start.19
  145.2 3.5 %copy-start.36 = (f32[392]{0:T(512)S(1)}, f32[392]{0:T(512)}, u32[]{:S(2)}) copy-start(f32[392]{0:T(512)} %copy-done.35) | copy-start | bytes 4708
  145.2 3.5 %copy-start.43 = (f32[512]{0:T(512)S(1)}, f32[512]{0:T(512)}, u32[]{:S(2)}) copy-start(f32[512]{0:T(512)} %param.18) | copy-start | bytes 6148
  145.2 3.5 %copy-start.57 = (f32[512]{0:T(512)S(1)}, f32[512]{0:T(512)}, u32[]{:S(2)}) copy-start(f32[512]{0:T(512)} %param.19) | copy-start | bytes 6148
  145.2 179.9 %all-reduce.12.cloned.1.call-start = ((), (), s32[]{:S(2)}) async-start(), calls=%async_computation.2 | async-start | bytes 12582912 | tf_op jit(solution)/shard_map/psum | solution.py:208
  150.6 0.9 copy-start.25
  150.6 1.4 copy-start.39
  150.7 31.1 %copy-start.44 = (f32[512]{0:T(512)S(1)}, f32[512]{0:T(512)}, u32[]{:S(2)}) copy-start(f32[512]{0:T(512)} %get-tuple-element.15) | copy-start | bytes 6148
  150.7 31.1 %copy-start.45 = (f32[512]{0:T(512)S(1)}, f32[512]{0:T(512)}, u32[]{:S(2)}) copy-start(f32[512]{0:T(512)} %get-tuple-element.21) | copy-start | bytes 6148
  150.7 31.1 %copy-start.46 = (f32[512]{0:T(512)S(1)}, f32[512]{0:T(512)}, u32[]{:S(2)}) copy-start(f32[512]{0:T(512)} %get-tuple-element.40) | copy-start | bytes 6148
  150.7 31.1 %copy-start.47 = (f32[512]{0:T(512)S(1)}, f32[512]{0:T(512)}, u32[]{:S(2)}) copy-start(f32[512]{0:T(512)} %get-tuple-element.54) | copy-start | bytes 6148
  150.7 31.1 %copy-start.48 = (f32[1024]{0:T(1024)S(1)}, f32[1024]{0:T(1024)}, u32[]{:S(2)}) copy-start(f32[1024]{0:T(1024)} %get-tuple-element.63) | copy-start | bytes 12292
  150.7 94.4 %copy-start.6 = (bf16[392,512]{1,0:T(8,128)(2,1)S(1)}, bf16[392,512]{1,0:T(8,128)(2,1)}, u32[]{:S(2)}) copy-start(bf16[392,512]{1,0:T(8,128)(2,1)} %all-reduce.8.cloned.1.call-done) | copy-start | bytes 1204228
  150.7 94.4 %copy-start.49 = (f32[512]{0:T(512)S(1)}, f32[512]{0:T(512)}, u32[]{:S(2)}) copy-start(f32[512]{0:T(512)} %param.32) | copy-start | bytes 6148
  325.1 2.8 copy-start.30
  325.1 3.6 %copy-start.17 = (f32[512,1024]{1,0:T(8,128)S(1)}, f32[512,1024]{1,0:T(8,128)}, u32[]{:S(2)}) copy-start(f32[512,1024]{1,0:T(8,128)} %get-tuple-element.92) | copy-start | bytes 6291460
  328.7 2.3 copy-start.16
  328.7 3.7 %copy-start.1 = (bf16[512,1024]{1,0:T(8,128)(2,1)S(1)}, bf16[512,1024]{1,0:T(8,128)(2,1)}, u32[]{:S(2)}) copy-start(bf16[512,1024]{1,0:T(8,128)(2,1)} %param.29) | copy-start | bytes 3145732
Sparse Core Ops, SparseCore 0:
  43.3 28.6 all-reduce.7
  80.5 26.1 all-reduce.9
  145.3 34.8 all-reduce.13
  185.2 139.8 all-reduce.11
where the time goes:
time: 340 us; the launch traced here: 339 us
  waiting for transfers between devices  154 us (45%)
  blocking collectives  63.3 us (19%)
  local copies, waits for them, and re-layouts  53.2 us (16%)
  matrix products  32 us (9%)
  other arithmetic  20.7 us (6%)
  between operations  14.7 us (4%)
    psum x1, waiting for transfers between devices, local(): lax.psum((grad_ln1_gain, grad_ln1_shift, grad_qkv, grad_qv_bias, grad_tab...  77.4 us
    psum x1, blocking collectives, local(): lax.psum((grad_ln1_gain, grad_ln1_shift, grad_qkv, grad_qv_bias, grad_tab...  63.3 us
    psum x1, waiting for transfers between devices, local(): lax.psum(attn_part.astype(jnp.bfloat16), 'tensor').astype(jnp.float32)  28.6 us
    psum x1, waiting for transfers between devices, local(): lax.psum(mlp_part.astype(jnp.bfloat16), 'tensor').astype(jnp.float32)  27.3 us
    psum x1, waiting for transfers between devices, local(): lax.psum(back_two_part.astype(jnp.bfloat16), 'tensor').astype(jnp.float32)  21 us
    unnamed x125, local copies, waits for them, and re-layouts  13.7 us
    reshape x4, local copies, waits for them, and re-layouts, to_windows(): layout.reshape(images * across * across, heads_here, WIN * WIN, head_depth)  7.54 us
  transfers between devices with their start and end apart: 4, of which 4 were waited for; matrix products, arithmetic and copies ran while one was open for 5% of the time, Pallas kernels for 0%

commit v1 on v0

--- a/solution.py
+++ b/solution.py
@@ -1,3 +1,4 @@
+import functools
 import jax
 import jax.numpy as jnp
 from jax import lax
@@ -9,6 +10,13 @@
 SHIFT = 3
 NORM_EPS = 1e-05
 MASKED = -1e30
+
+
+def floor_lift(x_local, which_axis):
+    return jnp.sum(lax.all_gather(x_local, which_axis), axis=0)
+
+
+step_on_ticks = functools.partial(floor_lift, which_axis="tensor")
 
 
 def layer_norm(values, norm_gain, norm_shift):
@@ -136,7 +144,7 @@
     mixed = jnp.einsum("whij,whje->whie", prob_b, value_win, preferred_element_type=jnp.float32)
     mixed_tok = from_windows(mixed.astype(jnp.bfloat16), images)
     attn_part = jnp.dot(mixed_tok, w_proj, preferred_element_type=jnp.float32)
-    attn_total = lax.psum(attn_part.astype(jnp.bfloat16), "tensor").astype(jnp.float32)
+    attn_total = step_on_ticks(attn_part.astype(jnp.bfloat16)).astype(jnp.float32)
     hidden_res = residual_in + attn_total + proj_bias
     normed_two, unit_two, inverse_two = layer_norm(hidden_res, ln2_gain, ln2_shift)
     normed_two_b = normed_two.astype(jnp.bfloat16)

time: 340 us -> 324 us (0.953)
  waiting for transfers between devices: 154 us -> 127 us
  blocking collectives: 63.3 us -> 76.5 us
    psum x1 -> x0, waiting for transfers between devices: 28.6 us -> none  [local(): lax.psum(attn_part.astype(jnp.bfloat16), 'tensor').astype(jnp.float32)]
    all_gather x0 -> x1, blocking collectives: none -> 13.2 us  [floor_lift(): return jnp.sum(lax.all_gather(x_local, which_axis), axis=0)]
    unnamed x125 -> x129, local copies, waits for them, and re-layouts: 13.7 us -> 14.6 us
  transfers between devices with their start and end apart: 4 -> 3, of which waited for: 4 -> 3; matrix products, arithmetic and copies ran while one was open for 5% -> 5% of each run, Pallas kernels for 0% -> 0%
where the time goes in v1:
time: 324 us; the launch traced here: 323 us
  waiting for transfers between devices  127 us (39%)
  blocking collectives  76.5 us (24%)
  local copies, waits for them, and re-layouts  53.3 us (16%)
  matrix products  30.2 us (9%)
  other arithmetic  20.6 us (6%)
  between operations  14.7 us (5%)
    psum x1, waiting for transfers between devices, local(): lax.psum((grad_ln1_gain, grad_ln1_shift, grad_qkv, grad_qv_bias, grad_tab...  77.6 us
    psum x1, blocking collectives, local(): lax.psum((grad_ln1_gain, grad_ln1_shift, grad_qkv, grad_qv_bias, grad_tab...  63.3 us
    psum x1, waiting for transfers between devices, local(): lax.psum(mlp_part.astype(jnp.bfloat16), 'tensor').astype(jnp.float32)  27.2 us
    psum x1, waiting for transfers between devices, local(): lax.psum(back_two_part.astype(jnp.bfloat16), 'tensor').astype(jnp.float32)  22.4 us
    unnamed x129, local copies, waits for them, and re-layouts  14.6 us
    all_gather x1, blocking collectives, floor_lift(): return jnp.sum(lax.all_gather(x_local, which_axis), axis=0)  13.2 us
    reshape x4, local copies, waits for them, and re-layouts, to_windows(): layout.reshape(images * across * across, heads_here, WIN * WIN, head_depth)  6.79 us
  transfers between devices with their start and end apart: 3, of which 3 were waited for; matrix products, arithmetic and copies ran while one was open for 5% of the time, Pallas kernels for 0%

profile of v1, /device:TPU:0, one launch (start us, length us, event | category | flops | bytes accessed | tf_op | source)
XLA Modules:
  0.0 322.9 jit_solution(7107853855783026210)
XLA Ops:
  7.3 1.2 convert_reduce_fusion.2
  8.5 1.2 fusion.26
  9.8 1.4 copy.96
  13.7 0.9 slice.167
  14.7 1.4 squeeze.7
  16.9 0.9 slice.162
  18.4 0.9 slice.172
  19.8 1.2 convolution_bitcast_fusion
  21.2 0.8 copy.101
  22.4 1.3 copy.100
  24.2 1.4 copy.99
  25.6 2.0 fusion.72
  29.0 0.9 copy.102
  29.9 2.4 copy.104
  32.3 2.2 convolution_convert_fusion
  34.6 2.4 copy.105
  37.0 1.2 copy.106
  38.3 1.1 fusion.35
  39.3 1.7 reshape.250
  41.1 1.3 convolution_convert_fusion.3
  42.4 13.2 %all-gather = bf16[784,512]{1,0:T(8,128)(2,1)} all-gather(bf16[392,512]{1,0:T(8,128)(2,1)S(1)} %convolution_convert_fusion.3), channel_id=2, replica_groups=mesh['dp'=16,'tensor'=2] {'tensor'}, dimensions={0}, use_global_device_ids=true | all-gather | bytes 1204224 | tf_op jit(solution)/shard_map/all_gather | solution.py:16
  55.6 2.1 reduce_sum.227
  57.8 1.3 fusion.55
  59.1 1.3 multiply_reduce_fusion.1
  60.4 1.8 multiply_convert_fusion
  62.2 1.6 fusion.73
  63.8 0.9 copy-done.60
  64.7 1.4 convolution_convert_fusion.1
  66.1 2.9 convolution_convert_fusion.2
  69.1 2.2 fusion.52
  71.3 22.4 %all-reduce.7.cloned.1.call-done = bf16[392,512]{1,0:T(8,128)(2,1)} async-done(((bf16[392,512]{1,0:T(8,128)(2,1)}), bf16[392,512]{1,0:T(8,128)(2,1)}) %all-reduce.7.cloned.1.call-update) | async-done | bytes 401424 | tf_op jit(solution)/shard_map/psum | solution.py:165
  93.7 1.6 fusion.32
  95.3 1.5 fusion.65
  96.8 0.9 copy-done.5
  98.0 1.2 reshape_reshape.2
  99.2 0.9 slice.179
  100.2 1.1 slice.178
  101.6 0.9 copy.107
  102.6 1.6 copy.108
  104.2 1.6 fusion.56
  105.8 3.0 copy.120
  108.8 1.5 copy.121
  111.2 1.1 slice.187
  113.0 1.3 fusion.66
  115.4 1.4 convolution_multiply_fusion
  117.4 0.9 slice.185
  118.3 1.9 copy.112
  120.5 1.2 copy-done.7
  123.8 1.2 stack_reshape.10
  126.5 2.5 fusion.8
  129.4 2.1 fusion.74
  131.5 1.1 fusion.59
  132.6 1.9 fusion.45
  134.6 0.9 copy-done.28
  136.0 0.9 fusion
  136.9 27.2 %all-reduce.11.cloned.1.call-done = (bf16[392,512]{1,0:T(8,128)(2,1)}, bf16[392,512]{1,0:T(8,128)(2,1)}) async-done(((bf16[392,512]{1,0:T(8,128)(2,1)}, bf16[392,512]{1,0:T(8,128)(2,1)}), (bf16[392,512]{1,0:T(8,128)(2,1)}, bf16[392,512]{1,0:T(8,128)(2,1)})) %all-reduce.11.cloned.1.call-update) | async-done | bytes 802832 | tf_op jit(solution)/shard_map/psum | solution.py:154
  164.1 1.5 fusion.33
  165.6 63.3 %all-reduce = (f32[512]{0:T(512)}, f32[512]{0:T(512)}, f32[2,256]{1,0:T(2,128)}, f32[169,8]{0,1:T(8,128)}, f32[512]{0:T(512)}, /*index=5*/f32[512]{0:T(512)}, f32[512]{0:T(512)}, f32[1024]{0:T(1024)}, f32[512]{0:T(512)}) all-reduce(f32[512]{0:T(512)S(1)} %get-tuple-element.17, ...), channel_id=1, replica_groups=mesh['dp'=16,'tensor'=2] {'dp'}, use_global_device_ids=true, to_apply=%region_16.17 | all-reduce | flops 5960 | bytes 47680 | tf_op jit(solution)/shard_map/psum | solution.py:216
  228.9 2.6 fusion.25
  231.5 77.6 %all-reduce.9.cloned.1.call-done = (f32[512,3,256]{2,0,1:T(8,128)}, f32[256,512]{1,0:T(8,128)}, f32[512,1024]{1,0:T(8,128)}, f32[1024,512]{1,0:T(8,128)}) async-done(((f32[512,3,256]{2,0,1:T(8,128)}, f32[256,512]{1,0:T(8,128)}, f32[512,1024]{1,0:T(8,128)}, f32[1024,512]{1,0:T(8,128)}), (f32[512,3,256]{2,0,1:T(8,128)}, f32[256,512]{1,0:T(8,128)}, f32[512,1024]{1,0:T(8,128)}, ...) | async-done | bytes 6291472 | tf_op jit(solution)/shard_map/psum | solution.py:216
  309.1 2.8 copy.145
  312.7 1.3 copy.147
  314.0 1.0 copy-done.18
  315.0 1.3 copy.148
  (192 shorter events, 16.2 us)
Async XLA Ops:
  7.2 53.2 %copy-start = (bf16[512,1024]{1,0:T(8,128)(2,1)S(1)}, bf16[512,1024]{1,0:T(8,128)(2,1)}, u32[]{:S(2)}) copy-start(bf16[512,1024]{1,0:T(8,128)(2,1)} %param.29) | copy-start | bytes 3145732
  7.2 4.0 %copy-start.2 = (bf16[392,512]{1,0:T(8,128)(2,1)S(1)}, bf16[392,512]{1,0:T(8,128)(2,1)}, u32[]{:S(2)}) copy-start(bf16[392,512]{1,0:T(8,128)(2,1)} %param.17) | copy-start | bytes 1204228
  7.2 4.0 %copy-start.48 = (f32[512]{0:T(512)S(1)}, f32[512]{0:T(512)}, u32[]{:S(2)}) copy-start(f32[512]{0:T(512)} %param.18) | copy-start | bytes 6148
  7.2 4.0 %copy-start.58 = (f32[512]{0:T(512)S(1)}, f32[512]{0:T(512)}, u32[]{:S(2)}) copy-start(f32[512]{0:T(512)} %param.19) | copy-start | bytes 6148
  7.2 86.5 %all-reduce.7.cloned.1.call-start = ((), (), s32[]{:S(2)}) async-start(), calls=%async_computation | async-start | bytes 802816 | tf_op jit(solution)/shard_map/psum | solution.py:165
  9.8 2.0 copy-start.41
  12.7 1.9 copy-start.52
  18.2 1.1 copy-start.40
  18.2 1.2 copy-start.53
  18.3 1.5 copy-start.55
  18.4 3.6 %copy-start.9 = (bf16[2,11,14,8,32]{4,3,2,1,0:T(8,128)(2,1)S(1)}, bf16[2,11,14,8,32]{4,3,2,1,0:T(8,128)(2,1)}, u32[]{:S(2)}) copy-start(bf16[2,11,14,8,32]{4,3,2,1,0:T(8,128)(2,1)} %slice.167) | copy-start | bytes 473092
  18.4 3.6 %copy-start.25 = (bf16[2,3,14,8,32]{4,3,2,1,0:T(8,128)(2,1)S(1)}, bf16[2,3,14,8,32]{4,3,2,1,0:T(8,128)(2,1)}, u32[]{:S(2)}) copy-start(bf16[2,3,14,8,32]{4,3,2,1,0:T(8,128)(2,1)} %slice.168) | copy-start | bytes 129028
  19.4 2.9 copy-start.44
  22.3 1.4 copy-start.10
  22.4 1.4 copy-start.26
  27.6 1.1 copy-start.8
  28.6 3.7 %copy-start.29 = (f32[8,8,49]{2,1,0:T(8,128)}, f32[8,8,49]{2,1,0:T(8,128)S(1)}, u32[]{:S(2)}) copy-start(f32[8,8,49]{2,1,0:T(8,128)S(1)} %log_add_fusion) | copy-start | bytes 37636
  41.1 16.7 %copy-start.20 = (bf16[392,256]{1,0:T(8,128)(2,1)}, bf16[392,256]{1,0:T(8,128)(2,1)S(1)}, u32[]{:S(2)}) copy-start(bf16[392,256]{1,0:T(8,128)(2,1)S(1)} %reshape.250) | copy-start | bytes 602116
  41.1 16.7 %copy-start.38 = (f32[512]{0:T(512)S(1)}, f32[512]{0:T(512)}, u32[]{:S(2)}) copy-start(f32[512]{0:T(512)} %param.26) | copy-start | bytes 6148
  55.6 4.8 %copy-start.46 = (f32[512]{0:T(512)S(1)}, f32[512]{0:T(512)}, u32[]{:S(2)}) copy-start(f32[512]{0:T(512)} %param.27) | copy-start | bytes 6148
  55.6 4.8 %copy-start.56 = (f32[1024]{0:T(1024)S(1)}, f32[1024]{0:T(1024)}, u32[]{:S(2)}) copy-start(f32[1024]{0:T(1024)} %param.30) | copy-start | bytes 12292
  55.6 4.8 %copy-start.57 = (f32[512]{0:T(512)S(1)}, f32[512]{0:T(512)}, u32[]{:S(2)}) copy-start(f32[512]{0:T(512)} %param.28) | copy-start | bytes 6148
  57.8 2.6 copy-start.3
  59.1 10.0 %copy-start.39 = (f32[392]{0:T(512)}, f32[392]{0:T(512)S(1)}, u32[]{:S(2)}) copy-start(f32[392]{0:T(512)S(1)} %broadcast_multiply_fusion.4) | copy-start | bytes 4708
  60.4 8.6 %copy-start.43 = (f32[392]{0:T(512)}, f32[392]{0:T(512)S(1)}, u32[]{:S(2)}) copy-start(f32[392]{0:T(512)S(1)} %add_rsqrt_fusion) | copy-start | bytes 4708
  60.4 1.8 copy-start.22
  60.4 1.8 copy-start.54
  66.1 3.0 copy-start.4
  66.1 98.0 %all-reduce.11.cloned.1.call-start = ((), (), s32[]{:S(2)}) async-start(), calls=%async_computation.2 | async-start | bytes 1605632 | tf_op jit(solution)/shard_map/psum | solution.py:154
  66.1 2.9 copy-start.61
  69.1 24.6 %copy-start.47 = (f32[512]{0:T(512)S(1)}, f32[512]{0:T(512)}, u32[]{:S(2)}) copy-start(f32[512]{0:T(512)} %param.27) | copy-start | bytes 6148
  69.1 26.2 %copy-start.23 = (bf16[392,512]{1,0:T(8,128)(2,1)S(1)}, bf16[392,512]{1,0:T(8,128)(2,1)}, u32[]{:S(2)}) copy-start(bf16[392,512]{1,0:T(8,128)(2,1)} %param.33) | copy-start | bytes 1204228
  71.3 26.4 %copy-start.27 = (bf16[256,512]{1,0:T(8,128)(2,1)S(1)}, bf16[256,512]{1,0:T(8,128)(2,1)}, u32[]{:S(2)}) copy-start(bf16[256,512]{1,0:T(8,128)(2,1)} %param.25) | copy-start | bytes 786436
  96.8 0.9 copy-start.5
  101.6 2.6 copy-start.30
  104.2 1.6 copy-start.14
  110.4 1.9 copy-start.13
  110.4 1.9 copy-start.15
  113.0 1.3 copy-start.12
  114.3 1.0 copy-start.11
  120.3 1.3 copy-start.7
  120.3 1.3 copy-start.16
  122.5 1.1 copy-start.17
  123.6 1.4 copy-start.33
  123.8 1.9 copy-start.32
  125.2 1.3 copy-start.35
  126.5 2.5 copy-start.36
  126.5 2.9 copy-start.24
  126.5 2.9 copy-start.31
  129.0 2.5 copy-start.6
  129.0 2.5 copy-start.21
  129.0 3.6 %copy-start.42 = (f32[392]{0:T(512)S(1)}, f32[392]{0:T(512)}, u32[]{:S(2)}) copy-start(f32[392]{0:T(512)} %copy-done.41) | copy-start | bytes 4708
  129.1 3.6 %copy-start.49 = (f32[512]{0:T(512)S(1)}, f32[512]{0:T(512)}, u32[]{:S(2)}) copy-start(f32[512]{0:T(512)} %param.18) | copy-start | bytes 6148
  129.1 3.6 %copy-start.59 = (f32[512]{0:T(512)S(1)}, f32[512]{0:T(512)}, u32[]{:S(2)}) copy-start(f32[512]{0:T(512)} %param.19) | copy-start | bytes 6148
  129.1 180.0 %all-reduce.9.cloned.1.call-start = ((), (), s32[]{:S(2)}) async-start(), calls=%async_computation.1 | async-start | bytes 12582912 | tf_op jit(solution)/shard_map/psum | solution.py:216
  129.4 3.3 %copy-start.37 = (bf16[392,1,256]{2,0,1:T(8,128)(2,1)S(1)}, bf16[392,1,256]{2,0,1:T(8,128)(2,1)}, u32[]{:S(2)}) copy-start(bf16[392,1,256]{2,0,1:T(8,128)(2,1)} %copy-done.36) | copy-start | bytes 602116
  134.6 0.9 copy-start.28
  134.6 1.4 copy-start.45
  134.6 31.0 %copy-start.50 = (f32[1024]{0:T(1024)S(1)}, f32[1024]{0:T(1024)}, u32[]{:S(2)}) copy-start(f32[1024]{0:T(1024)} %get-tuple-element.63) | copy-start | bytes 12292
  134.6 94.3 %copy-start.51 = (f32[512]{0:T(512)S(1)}, f32[512]{0:T(512)}, u32[]{:S(2)}) copy-start(f32[512]{0:T(512)} %param.32) | copy-start | bytes 6148
  309.1 2.8 copy-start.34
  309.1 3.6 %copy-start.19 = (f32[512,1024]{1,0:T(8,128)S(1)}, f32[512,1024]{1,0:T(8,128)}, u32[]{:S(2)}) copy-start(f32[512,1024]{1,0:T(8,128)} %get-tuple-element.92) | copy-start | bytes 6291460
  312.7 2.3 copy-start.18
  312.7 3.7 %copy-start.1 = (bf16[512,1024]{1,0:T(8,128)(2,1)S(1)}, bf16[512,1024]{1,0:T(8,128)(2,1)}, u32[]{:S(2)}) copy-start(bf16[512,1024]{1,0:T(8,128)(2,1)} %param.29) | copy-start | bytes 3145732
  (1 other events, 0.9 us)
Sparse Core Ops, SparseCore 0:
  66.2 27.4 all-reduce.6
  129.1 34.8 all-reduce.10
  169.2 139.8 all-reduce.8
